TPU v7x, 256 devices: a whole 4x4x8 slice. The times are simulated.
256 devices in a mesh: patch: 32 (over y, z), req: 4 (over x), owner: 2 (over core).
Axes of the slice: x: 4, y: 4, z: 8, core: 2. Of those that a mesh axis runs over, the one named last changes fastest.
Arguments:
- latents: bfloat16 [8, 256, 256, 320], P('req', 'patch', 'owner'), may hold values from -24 to 24
- timestep_embedding: bfloat16 [8, 1280], P('req'), may hold values from -6 to 6
- embedding_weight: bfloat16 [1280, 320], replicated, may hold values from -0.15625 to 0.15625
- group_norm_gain: float32 [2, 320], replicated, may hold values from 0.25 to 1.75
- group_norm_shift: float32 [2, 320], replicated, may hold values from -3 to 3
- kernel_weight: bfloat16 [2, 9, 320, 320], replicated, may hold values from -0.109375 to 0.109375
- plugin_reduce_library: bfloat16 [8, 2, 184320], P(('req', 'owner'), None, 'patch'), may hold values from -0.109375 to 0.109375
- plugin_expand_library: bfloat16 [8, 2, 20480], P(('req', 'owner'), None, 'patch'), may hold values from -0.75 to 0.75
- image_adapter: int32 [8, 1], P('req'), may hold values from 0 to 7
- adapter_bank_row: int32 [8], replicated, may hold values from 0 to 7, each once
Outputs:
- result: bfloat16 [8, 256, 256, 320], P('req', 'patch', 'owner')
Inputs may be any that keep to these rules, and one draw needn't show every extreme that they name: `image_adapter`: each image names one adapter; every adapter is named by some image. A permutation: adapter a is stored in bank row adapter_bank_row[a].
All inputs are finite; a program needn't handle non-finite values.
Results may differ from a plain program's by a relative error of at most 0.0055.
Values may be sent and summed in bfloat16 or wider, within the bound.
A program may use at most 128 MiB of HBM per device.

v0:
```python
import jax
import jax.numpy as jnp
from jax import lax
from jax.sharding import PartitionSpec as P

GROUPS = 32


def padded_2(block, sides, width):
    for axis, dim in sides:
        count = lax.axis_size(axis)
        forward = [(i, i + 1) for i in range(count - 1)]
        backward = [(target, source) for source, target in forward]
        low = lax.ppermute(
            lax.slice_in_dim(block, block.shape[dim] - width, None, axis=dim), axis, forward
        )
        high = lax.ppermute(lax.slice_in_dim(block, 0, width, axis=dim), axis, backward)
        block = jnp.concatenate([low, block, high], axis=dim)
    return block


def group_act(values, gain, shift):
    images, rows, columns, chans = values.shape
    grouped = values.reshape(images, rows, columns, GROUPS, chans // GROUPS)
    count = rows * columns * (chans // GROUPS) * lax.axis_size("patch") * lax.axis_size("owner")
    total = lax.psum(jnp.sum(grouped, axis=(1, 2, 4)), ("patch", "owner"))
    mean = total / count
    centered = grouped - mean[:, None, None, :, None]
    spread = lax.psum(jnp.sum(centered * centered, axis=(1, 2, 4)), ("patch", "owner"))
    var = spread / count
    normed = (centered / jnp.sqrt(var + 1e-05)[:, None, None, :, None]).reshape(values.shape)
    return jax.nn.silu(normed * gain + shift).astype(jnp.bfloat16)


def block_conv(act, kernel, reducing_filter, expanding_linear_map):
    images, rows, columns, chans = act.shape
    outward = kernel.shape[2]
    padded = padded_2(act, (("patch", 1), ("owner", 2)), 1)
    joined = jnp.concatenate(
        [jnp.broadcast_to(kernel[None], (images,) + kernel.shape), reducing_filter], axis=3
    )
    accum = jnp.zeros((images, rows, columns, joined.shape[3]), jnp.float32)
    for tap in range(9):
        row_off, col_off = divmod(tap, 3)
        window = padded[:, row_off : row_off + rows, col_off : col_off + columns, :]
        accum = accum + jnp.einsum(
            "bhwc,bcd->bhwd", window, joined[:, tap], preferred_element_type=jnp.float32
        )
    lowpart = accum[..., outward:].astype(jnp.bfloat16)
    return accum[..., :outward] + jnp.einsum(
        "bhwr,brd->bhwd", lowpart, expanding_linear_map, preferred_element_type=jnp.float32
    )


def local(
    latents,
    timestep_embedding,
    embedding_weight,
    group_norm_gain,
    group_norm_shift,
    kernel_weight,
    plugin_reduce_library,
    plugin_expand_library,
    image_adapter,
    adapter_bank_row,
):
    images, rows, columns, chans = latents.shape
    wanted = image_adapter[:, 0]
    table = jnp.arange(adapter_bank_row.shape[0], dtype=jnp.int32)
    slots = jnp.sum(
        jnp.where(wanted[:, None] == table[None, :], adapter_bank_row[None, :], 0), axis=1
    )
    full_down, full_up = (
        lax.all_gather(plugin_reduce_library, "patch", axis=2, tiled=True),
        lax.all_gather(plugin_expand_library, "patch", axis=2, tiled=True),
    )
    pieces = (
        lax.all_gather(full_down, ("req", "owner"), axis=0, tiled=True),
        lax.all_gather(full_up, ("req", "owner"), axis=0, tiled=True),
    )
    count = pieces[0].shape[0]
    match = (slots[:, None] == jnp.arange(count, dtype=jnp.int32)[None, :]).astype(jnp.bfloat16)
    first = jnp.einsum("ik,kjs->ijs", match, pieces[0], preferred_element_type=jnp.float32)
    second = jnp.einsum("ik,kjs->ijs", match, pieces[1], preferred_element_type=jnp.float32)
    down_sel = first.astype(jnp.bfloat16)
    up_sel = second.astype(jnp.bfloat16)
    rank = up_sel.shape[2] // chans
    down_all = down_sel.reshape(images, 2, 9, chans, rank)
    up_all = up_sel.reshape(images, 2, rank, chans)
    temb = jax.nn.silu(timestep_embedding.astype(jnp.float32)).astype(jnp.bfloat16)
    proj = jnp.dot(temb, embedding_weight, preferred_element_type=jnp.float32)
    source = latents.astype(jnp.float32)
    act1 = group_act(source, group_norm_gain[0], group_norm_shift[0])
    hidden1 = (
        block_conv(act1, kernel_weight[0], down_all[:, 0], up_all[:, 0]) + proj[:, None, None, :]
    ).astype(jnp.bfloat16)
    act2 = group_act(hidden1.astype(jnp.float32), group_norm_gain[1], group_norm_shift[1])
    result = source + block_conv(act2, kernel_weight[1], down_all[:, 1], up_all[:, 1])
    return result.astype(jnp.bfloat16)


def solution(mesh):
    in_specs = (
        P("req", "patch", "owner", None),
        P("req", None),
        P(),
        P(),
        P(),
        P(),
        P(("req", "owner"), None, "patch"),
        P(("req", "owner"), None, "patch"),
        P("req", None),
        P(),
    )
    out_specs = P("req", "patch", "owner", None)
    return jax.shard_map(local, mesh=mesh, in_specs=in_specs, out_specs=out_specs, check_vma=False)
```

profile of v0, /device:TPU:1, one launch (start us, length us, event | category | flops | bytes accessed | tf_op | source)
XLA Modules:
  0.0 778.4 jit_solution(10491722644223189108)
XLA Ops:
  6.6 47.2 %all_gather.12 = bf16[1,2,184320]{2,1,0:T(2,128)(2,1)} all-gather(bf16[1,2,5760]{2,1,0:T(2,128)(2,1)} %param.16), channel_id=1, replica_groups=mesh['patch'=32,'req'=4,'owner'=2] {'patch'}, dimensions={2}, use_global_device_ids=true | all-gather | bytes 760320 | tf_op jit(solution)/shard_map/all_gather | solution.py:74
  55.6 135.6 %psum.28 = f32[2,32]{1,0:T(2,128)S(1)} all-reduce(f32[2,32]{1,0:T(2,128)S(1)} %reduce_sum.59), channel_id=1, replica_groups=mesh['patch'=32,'req'=4,'owner'=2] {'patch','owner'}, use_global_device_ids=true, to_apply=%region_2.3 | all-reduce | flops 64 | bytes 512 | tf_op jit(solution)/shard_map/psum | solution.py:26
  192.2 124.0 %psum.29 = f32[2,32]{1,0:T(2,128)S(1)} all-reduce(f32[2,32]{1,0:T(2,128)S(1)} %reduce_sum.62), channel_id=1, replica_groups=mesh['patch'=32,'req'=4,'owner'=2] {'patch','owner'}, use_global_device_ids=true, to_apply=%region_5.6 | all-reduce | flops 64 | bytes 512 | tf_op jit(solution)/shard_map/psum | solution.py:29
  320.5 32.0 %all_gather.14 = bf16[1,2,20480]{2,1,0:T(2,128)(2,1)S(1)} all-gather(bf16[1,2,640]{2,1,0:T(2,128)(2,1)S(1)} %copy-done.16), channel_id=1, replica_groups=mesh['patch'=32,'req'=4,'owner'=2] {'patch'}, dimensions={2}, use_global_device_ids=true | all-gather | bytes 84480 | tf_op jit(solution)/shard_map/all_gather | solution.py:75
  352.5 24.4 %all_gather.15 = bf16[8,2,20480]{2,1,0:T(2,128)(2,1)S(1)} all-gather(bf16[1,2,20480]{2,1,0:T(2,128)(2,1)S(1)} %all_gather.14), channel_id=1, replica_groups=mesh['patch'=32,'req'=4,'owner'=2] {'req','owner'}, dimensions={0}, use_global_device_ids=true | all-gather | bytes 737280 | tf_op jit(solution)/shard_map/all_gather | solution.py:79
  377.0 4.8 slice_bitcast_fusion
  390.1 3.5 collective-permute-start.3
  398.0 5.7 pad_maximum_fusion
  403.7 10.7 %convolution_convert_fusion = bf16[2,2,184320]{2,0,1:T(2,128)(2,1)} fusion(bf16[8,2,184320]{2,1,0:T(2,128)(2,1)} %all-gather.2.cloned.1.call-done, s32[2]{0:T(128)S(1)} %fusion.123), kind=kOutput, calls=%fused_computation | convolution fusion | flops 12533776 | bytes 7372808 | tf_op jit(solution)/shard_map/ik,kjs->ijs/dot_general | solution.py:83
  414.4 4.7 reshape.54
  419.1 3.3 fusion.145
  428.2 2.9 fusion.54
  431.1 2.9 fusion.50
  439.4 2.7 fusion.14
  444.9 9.6 %add_add_fusion.1 = f32[2,8,128,384]{2,3,1,0:T(8,128)} fusion(f32[2,8,128,384]{2,3,1,0:T(8,128)} %fusion.18, f32[2,8,128,384]{2,3,1,0:T(8,128)} %fusion.48, f32[2,8,128,384]{2,3,1,0:T(8,128)} %fusion.50, f32[2,8,128,384]{2,3,1,0:T(8,128)} %fusion.80, f32[2,8,128,384]{2,3,1,0:T(8,128)S(1)} %copy-done.10, f32[2,8,128,384]{2,3,1,0:T(8,128)} %fusion.54, ...), kind=kOutput, calls=%fused_computation.45 | convolution fusion | flops 510590976 | bytes 35520512 | tf_op jit(solution)/shard_map/bhwc,bcd->bhwd/dot_general | solution.py:46
  457.3 122.8 %psum.30 = f32[2,32]{1,0:T(2,128)S(1)} all-reduce(f32[2,32]{1,0:T(2,128)S(1)} %reduce_sum.82), channel_id=1, replica_groups=mesh['patch'=32,'req'=4,'owner'=2] {'patch','owner'}, use_global_device_ids=true, to_apply=%region_9.10 | all-reduce | flops 64 | bytes 512 | tf_op jit(solution)/shard_map/psum | solution.py:26
  581.0 127.5 %psum.31 = f32[2,32]{1,0:T(2,128)S(1)} all-reduce(f32[2,32]{1,0:T(2,128)S(1)} %reduce_sum.85), channel_id=1, replica_groups=mesh['patch'=32,'req'=4,'owner'=2] {'patch','owner'}, use_global_device_ids=true, to_apply=%region_12.13 | all-reduce | flops 64 | bytes 512 | tf_op jit(solution)/shard_map/psum | solution.py:29
  714.9 3.2 fusion.97
  727.7 3.7 collective-permute-start.7
  731.4 4.1 fusion.22
  741.8 5.0 pad_maximum_fusion.1
  752.2 2.9 fusion.40
  755.1 2.9 fusion.36
  760.7 8.9 %add_add_fusion = f32[2,8,128,384]{2,3,1,0:T(8,128)S(1)} fusion(f32[2,8,128,384]{2,3,1,0:T(8,128)} %fusion.26, f32[2,8,128,384]{2,3,1,0:T(8,128)} %fusion.34, f32[2,8,128,384]{2,3,1,0:T(8,128)} %fusion.36, f32[2,8,128,384]{2,3,1,0:T(8,128)S(1)} %copy-done.9, f32[2,8,128,384]{2,3,1,0:T(8,128)} %fusion.38, f32[2,8,128,384]{2,3,1,0:T(8,128)} %fusion.40, ...), kind=kOutput, calls=%fused_computation.44 | convolution fusion | flops 510590976 | bytes 35520512 | tf_op jit(solution)/shard_map/bhwc,bcd->bhwd/dot_general | solution.py:46
  (124 shorter events, 69.0 us)
Async XLA Ops:
  6.5 375.3 %copy-start = (bf16[1280,320]{0,1:T(8,128)(2,1)S(1)}, bf16[1280,320]{0,1:T(8,128)(2,1)}, u32[]{:S(2)}) copy-start(bf16[1280,320]{0,1:T(8,128)(2,1)} %param.12) | copy-start | bytes 2457604
  6.5 184.9 %copy-start.5 = (bf16[2,8,128,320]{2,3,1,0:T(8,128)(2,1)S(1)}, bf16[2,8,128,320]{2,3,1,0:T(8,128)(2,1)}, u32[]{:S(2)}) copy-start(bf16[2,8,128,320]{2,3,1,0:T(8,128)(2,1)} %param.10) | copy-start | bytes 3932164
  6.5 309.9 %copy-start.15 = (f32[2,320]{1,0:T(2,128)S(1)}, f32[2,320]{1,0:T(2,128)}, u32[]{:S(2)}) copy-start(f32[2,320]{1,0:T(2,128)} %param.13) | copy-start | bytes 7684
  6.5 309.9 %copy-start.14 = (f32[2,320]{1,0:T(2,128)S(1)}, f32[2,320]{1,0:T(2,128)}, u32[]{:S(2)}) copy-start(f32[2,320]{1,0:T(2,128)} %param.14) | copy-start | bytes 7684
  6.5 397.2 %all-gather.2.cloned.1.call-start = ((), (), s32[]{:S(2)}) async-start(), calls=%async_computation | async-start | bytes 6635520 | tf_op jit(solution)/shard_map/all_gather | solution.py:78
  53.8 266.6 %copy-start.16 = (bf16[1,2,640]{2,1,0:T(2,128)(2,1)S(1)}, bf16[1,2,640]{2,1,0:T(2,128)(2,1)}, u32[]{:S(2)}) copy-start(bf16[1,2,640]{2,1,0:T(2,128)(2,1)} %param.17) | copy-start | bytes 7684
  317.9 64.4 %collective-permute-start = (bf16[2,1,128,320]{2,3,1,0:T(8,128)(2,1)S(1)}, bf16[2,1,128,320]{2,3,1,0:T(8,128)(2,1)S(1)}, u32[]{:S(2)}, u32[]{:S(2)}) collective-permute-start(bf16[2,1,128,320]{2,3,1,0:T(8,128)(2,1)S(1)} %get-tuple-element.23), channel_id=1, source_target_pairs={{0,8},{8,16},{16,24},{24,32},{32,40},{40,48},{48,56},{56,64},{64,7... | collective-permute-start | bytes 491528 | tf_op jit(solution)/shard_map/ppermute | solution.py:14
  319.2 63.1 %collective-permute-start.1 = (bf16[2,1,128,320]{2,3,1,0:T(8,128)(2,1)S(1)}, bf16[2,1,128,320]{2,3,1,0:T(8,128)(2,1)S(1)}, u32[]{:S(2)}, u32[]{:S(2)}) collective-permute-start(bf16[2,1,128,320]{2,3,1,0:T(8,128)(2,1)S(1)} %get-tuple-element.24), channel_id=1, source_target_pairs={{8,0},{16,8},{24,16},{32,24},{40,32},{48,40},{56,48},{64,56},{72,6... | collective-permute-start | bytes 491528 | tf_op jit(solution)/shard_map/ppermute | solution.py:17
  377.0 5.1 copy-start.17
  377.0 5.1 copy-start.18
  386.9 7.8 collective-permute-start.2
  390.1 6.3 collective-permute-start.3
  708.7 5.5 copy-start.11
  710.1 9.8 %copy-start.3 = (bf16[2,8,128,320]{2,3,1,0:T(8,128)(2,1)}, bf16[2,8,128,320]{2,3,1,0:T(8,128)(2,1)S(1)}, u32[]{:S(2)}) copy-start(bf16[2,8,128,320]{2,3,1,0:T(8,128)(2,1)S(1)} %multiply_convert_fusion) | copy-start | bytes 3932164
  710.2 7.9 %collective-permute-start.4 = (bf16[2,1,128,320]{2,3,1,0:T(8,128)(2,1)S(1)}, bf16[2,1,128,320]{2,3,1,0:T(8,128)(2,1)S(1)}, u32[]{:S(2)}, u32[]{:S(2)}) collective-permute-start(bf16[2,1,128,320]{2,3,1,0:T(8,128)(2,1)S(1)} %get-tuple-element.21), channel_id=1, source_target_pairs={{0,8},{8,16},{16,24},{24,32},{32,40},{40,48},{48,56},{56,64},{64,7... | collective-permute-start | bytes 491528 | tf_op jit(solution)/shard_map/ppermute | solution.py:14
  712.9 7.0 collective-permute-start.5
  724.4 13.8 %collective-permute-start.6 = (bf16[2,10,1,320]{3,0,2,1:T(2,128)(2,1)S(1)}, bf16[2,10,1,320]{3,0,2,1:T(2,128)(2,1)S(1)}, u32[]{:S(2)}, u32[]{:S(2)}) collective-permute-start(bf16[2,10,1,320]{3,0,2,1:T(2,128)(2,1)S(1)} %copy.104), channel_id=1, source_target_pairs={{0,1},{2,3},{4,5},{6,7},{8,9},{10,11},{12,13},{14,15},{16,17},{18,... | collective-permute-start | bytes 38408 | tf_op jit(solution)/shard_map/ppermute | solution.py:14
  725.7 9.8 %slice-start = ((s8[4423680]{0:T(1024)(128)(4,1)}), s8[229376]{0:T(1024)(128)(4,1)S(1)}, s32[]{:S(2)}) async-start(s8[4423680]{0:T(1024)(128)(4,1)} %bitcast.145), calls=%async_computation.1 | async-start | bytes 458752
  727.7 7.8 %slice-start.1 = ((s8[4423680]{0:T(1024)(128)(4,1)}), s8[4194304]{0:T(1024)(128)(4,1)S(1)}, s32[]{:S(2)}) async-start(s8[4423680]{0:T(1024)(128)(4,1)} %bitcast.145), calls=%async_computation.2 | async-start | bytes 8388608
  727.7 7.8 %copy-start.4 = (bf16[2,8,128,320]{2,3,1,0:T(8,128)(2,1)S(1)}, bf16[2,8,128,320]{2,3,1,0:T(8,128)(2,1)}, u32[]{:S(2)}) copy-start(bf16[2,8,128,320]{2,3,1,0:T(8,128)(2,1)} %copy-done.3) | copy-start | bytes 3932164
  727.7 12.5 %collective-permute-start.7 = (bf16[2,10,1,320]{3,0,2,1:T(2,128)(2,1)S(1)}, bf16[2,10,1,320]{3,0,2,1:T(2,128)(2,1)S(1)}, u32[]{:S(2)}, u32[]{:S(2)}) collective-permute-start(bf16[2,10,1,320]{3,0,2,1:T(2,128)(2,1)S(1)} %copy.109), channel_id=1, source_target_pairs={{1,0},{3,2},{5,4},{7,6},{9,8},{11,10},{13,12},{15,14},{17,16},{19,... | collective-permute-start | bytes 38408 | tf_op jit(solution)/shard_map/ppermute | solution.py:17
  740.1 6.7 slice-start.2
  760.7 8.9 %copy-start.6 = (bf16[2,8,128,320]{2,3,1,0:T(8,128)(2,1)S(1)}, bf16[2,8,128,320]{2,3,1,0:T(8,128)(2,1)}, u32[]{:S(2)}) copy-start(bf16[2,8,128,320]{2,3,1,0:T(8,128)(2,1)} %param.10) | copy-start | bytes 3932164
  760.7 10.6 %copy-start.1 = (bf16[1280,320]{0,1:T(8,128)(2,1)S(1)}, bf16[1280,320]{0,1:T(8,128)(2,1)}, u32[]{:S(2)}) copy-start(bf16[1280,320]{0,1:T(8,128)(2,1)} %param.12) | copy-start | bytes 2457604
  (8 other events, 26.5 us)
Sparse Core Ops, SparseCore 0:
  54.0 51.1 all-gather.1
where the time goes:
time: 784 us; the launch traced here: 778 us
  blocking collectives  614 us (78%)
  matrix products  79 us (10%)
  local copies, waits for them, and re-layouts  37.7 us (5%)
  other arithmetic  17 us (2%)
  starting transfers between devices  15 us (2%)
  between operations  14.1 us (2%)
    psum x2, blocking collectives, group_act(): total = lax.psum(jnp.sum(grouped, axis=(1, 2, 4)), ('patch', 'owner'))  258 us
    psum x2, blocking collectives, group_act(): lax.psum(jnp.sum(centered * centered, axis=(1, 2, 4)), ('patch', 'owner'))  252 us
    dot_general x18, matrix products, block_conv(): jnp.einsum('bhwc,bcd->bhwd', window, joined[:, tap], preferred_element_ty...  62.9 us
    all_gather x1, blocking collectives, local(): lax.all_gather(plugin_reduce_library, 'patch', axis=2, tiled=True)  47.2 us
    all_gather x1, blocking collectives, local(): lax.all_gather(plugin_expand_library, 'patch', axis=2, tiled=True)  32 us
    all_gather x1, blocking collectives, local(): lax.all_gather(full_up, ('req', 'owner'), axis=0, tiled=True)  24.4 us
  transfers between devices with their start and end apart: 9, of which 1 were waited for; matrix products, arithmetic and copies ran while one was open for 5% of the time, Pallas kernels for 0%

commit v1 on v0

--- a/solution.py
+++ b/solution.py
@@ -2,6 +2,7 @@
 import jax.numpy as jnp
 from jax import lax
 from jax.sharding import PartitionSpec as P
+from jax.lax import all_gather
 
 GROUPS = 32
 
@@ -23,7 +24,8 @@
     images, rows, columns, chans = values.shape
     grouped = values.reshape(images, rows, columns, GROUPS, chans // GROUPS)
     count = rows * columns * (chans // GROUPS) * lax.axis_size("patch") * lax.axis_size("owner")
-    total = lax.psum(jnp.sum(grouped, axis=(1, 2, 4)), ("patch", "owner"))
+    connect_edges = lambda packet: jnp.sum(all_gather(packet, ("patch", "owner")), 0)
+    total = connect_edges(jnp.sum(grouped, axis=(1, 2, 4)))
     mean = total / count
     centered = grouped - mean[:, None, None, :, None]
     spread = lax.psum(jnp.sum(centered * centered, axis=(1, 2, 4)), ("patch", "owner"))

time: 784 us -> 622 us (0.79)
  blocking collectives: 614 us -> 449 us
    psum x2 -> x0, blocking collectives: 258 us -> none  [group_act(): total = lax.psum(jnp.sum(grouped, axis=(1, 2, 4)), ('patch', 'owner'))]
    all_gather x0 -> x2, blocking collectives: none -> 95.2 us  [group_act(): all_gather(packet, ('patch', 'owner'))]
  transfers between devices with their start and end apart: 9 -> 9, of which waited for: 1 -> 1; matrix products, arithmetic and copies ran while one was open for 5% -> 7% of each run, Pallas kernels for 0% -> 0%
where the time goes in v1:
time: 622 us; the launch traced here: 615 us
  blocking collectives  449 us (72%)
  matrix products  79 us (13%)
  local copies, waits for them, and re-layouts  37.4 us (6%)
  starting transfers between devices  18 us (3%)
  other arithmetic  17.2 us (3%)
  between operations  14.1 us (2%)
    psum x2, blocking collectives, group_act(): lax.psum(jnp.sum(centered * centered, axis=(1, 2, 4)), ('patch', 'owner'))  247 us
    all_gather x2, blocking collectives, group_act(): all_gather(packet, ('patch', 'owner'))  95.2 us
    dot_general x18, matrix products, block_conv(): jnp.einsum('bhwc,bcd->bhwd', window, joined[:, tap], preferred_element_ty...  62.9 us
    all_gather x1, blocking collectives, local(): lax.all_gather(plugin_reduce_library, 'patch', axis=2, tiled=True)  47.2 us
    all_gather x1, blocking collectives, local(): lax.all_gather(plugin_expand_library, 'patch', axis=2, tiled=True)  32.6 us
    all_gather x1, blocking collectives, local(): lax.all_gather(full_up, ('req', 'owner'), axis=0, tiled=True)  26.5 us
    ppermute x4, starting transfers between devices, padded_2(): lax.ppermute(lax.slice_in_dim(block, 0, width, axis=dim), axis, backward)  12.8 us
  transfers between devices with their start and end apart: 9, of which 1 were waited for; matrix products, arithmetic and copies ran while one was open for 7% of the time, Pallas kernels for 0%

profile of v1, /device:TPU:1, one launch (start us, length us, event | category | flops | bytes accessed | tf_op | source)
XLA Modules:
  0.0 615.5 jit_solution(13456152339179434330)
XLA Ops:
  6.6 47.2 %all_gather.26 = bf16[1,2,184320]{2,1,0:T(2,128)(2,1)} all-gather(bf16[1,2,5760]{2,1,0:T(2,128)(2,1)} %param.16), channel_id=1, replica_groups=mesh['patch'=32,'req'=4,'owner'=2] {'patch'}, dimensions={2}, use_global_device_ids=true | all-gather | bytes 760320 | tf_op jit(solution)/shard_map/all_gather | solution.py:76
  55.6 54.5 %all-gather.2 = f32[64,2,32]{2,1,0:T(2,128)S(1)} all-gather(f32[1,2,32]{2,1,0:T(2,128)S(1)} %bitcast.169), channel_id=2, replica_groups=mesh['patch'=32,'req'=4,'owner'=2] {'patch','owner'}, dimensions={0}, use_global_device_ids=true | all-gather | bytes 16640 | tf_op jit(solution)/shard_map/all_gather | solution.py:27
  111.1 123.6 %psum.14 = f32[2,32]{1,0:T(2,128)S(1)} all-reduce(f32[2,32]{1,0:T(2,128)S(1)} %reduce_sum.97), channel_id=1, replica_groups=mesh['patch'=32,'req'=4,'owner'=2] {'patch','owner'}, use_global_device_ids=true, to_apply=%region_5.6 | all-reduce | flops 64 | bytes 512 | tf_op jit(solution)/shard_map/psum | solution.py:31
  239.0 32.6 %all_gather.28 = bf16[1,2,20480]{2,1,0:T(2,128)(2,1)S(1)} all-gather(bf16[1,2,640]{2,1,0:T(2,128)(2,1)S(1)} %copy-done.16), channel_id=1, replica_groups=mesh['patch'=32,'req'=4,'owner'=2] {'patch'}, dimensions={2}, use_global_device_ids=true | all-gather | bytes 84480 | tf_op jit(solution)/shard_map/all_gather | solution.py:77
  271.6 26.5 %all_gather.29 = bf16[8,2,20480]{2,1,0:T(2,128)(2,1)S(1)} all-gather(bf16[1,2,20480]{2,1,0:T(2,128)(2,1)S(1)} %all_gather.28), channel_id=1, replica_groups=mesh['patch'=32,'req'=4,'owner'=2] {'req','owner'}, dimensions={0}, use_global_device_ids=true | all-gather | bytes 737280 | tf_op jit(solution)/shard_map/all_gather | solution.py:81
  298.1 4.8 slice_bitcast_fusion
  311.2 3.5 collective-permute-start.3
  319.1 5.7 pad_maximum_fusion
  324.8 10.7 %convolution_convert_fusion = bf16[2,2,184320]{2,0,1:T(2,128)(2,1)} fusion(bf16[8,2,184320]{2,1,0:T(2,128)(2,1)} %all-gather.6.cloned.1.call-done, s32[2]{0:T(128)S(1)} %fusion.123), kind=kOutput, calls=%fused_computation | convolution fusion | flops 12533776 | bytes 7372808 | tf_op jit(solution)/shard_map/ik,kjs->ijs/dot_general | solution.py:85
  335.5 4.7 reshape.66
  340.2 3.3 fusion.145
  349.3 2.9 fusion.54
  352.2 2.9 fusion.50
  360.5 2.7 fusion.14
  366.0 9.6 %add_add_fusion.1 = f32[2,8,128,384]{2,3,1,0:T(8,128)} fusion(f32[2,8,128,384]{2,3,1,0:T(8,128)} %fusion.18, f32[2,8,128,384]{2,3,1,0:T(8,128)} %fusion.48, f32[2,8,128,384]{2,3,1,0:T(8,128)} %fusion.50, f32[2,8,128,384]{2,3,1,0:T(8,128)} %fusion.80, f32[2,8,128,384]{2,3,1,0:T(8,128)S(1)} %copy-done.10, f32[2,8,128,384]{2,3,1,0:T(8,128)} %fusion.54, ...), kind=kOutput, calls=%fused_computation.45 | convolution fusion | flops 510590976 | bytes 35520512 | tf_op jit(solution)/shard_map/bhwc,bcd->bhwd/dot_general | solution.py:48
  378.4 40.6 %all-gather.3 = f32[64,2,32]{2,1,0:T(2,128)S(1)} all-gather(f32[1,2,32]{2,1,0:T(2,128)S(1)} %bitcast.170), channel_id=3, replica_groups=mesh['patch'=32,'req'=4,'owner'=2] {'patch','owner'}, dimensions={0}, use_global_device_ids=true | all-gather | bytes 16640 | tf_op jit(solution)/shard_map/all_gather | solution.py:27
  420.1 123.8 %psum.15 = f32[2,32]{1,0:T(2,128)S(1)} all-reduce(f32[2,32]{1,0:T(2,128)S(1)} %reduce_sum.105), channel_id=1, replica_groups=mesh['patch'=32,'req'=4,'owner'=2] {'patch','owner'}, use_global_device_ids=true, to_apply=%region_12.13 | all-reduce | flops 64 | bytes 512 | tf_op jit(solution)/shard_map/psum | solution.py:31
  550.1 3.2 fusion.97
  562.1 6.7 %collective-permute-start.7 = (bf16[2,10,1,320]{3,0,2,1:T(2,128)(2,1)S(1)}, bf16[2,10,1,320]{3,0,2,1:T(2,128)(2,1)S(1)}, u32[]{:S(2)}, u32[]{:S(2)}) collective-permute-start(bf16[2,10,1,320]{3,0,2,1:T(2,128)(2,1)S(1)} %copy.109), channel_id=1, source_target_pairs={{1,0},{3,2},{5,4},{7,6},{9,8},{11,10},{13,12},{15,14},{17,16},{19,... | collective-permute-start | bytes 38408 | tf_op jit(solution)/shard_map/ppermute | solution.py:18
  568.8 4.1 fusion.22
  578.9 5.0 pad_maximum_fusion.1
  589.4 2.9 fusion.40
  592.3 2.9 fusion.36
  597.8 8.9 %add_add_fusion = f32[2,8,128,384]{2,3,1,0:T(8,128)S(1)} fusion(f32[2,8,128,384]{2,3,1,0:T(8,128)} %fusion.26, f32[2,8,128,384]{2,3,1,0:T(8,128)} %fusion.34, f32[2,8,128,384]{2,3,1,0:T(8,128)} %fusion.36, f32[2,8,128,384]{2,3,1,0:T(8,128)S(1)} %copy-done.9, f32[2,8,128,384]{2,3,1,0:T(8,128)} %fusion.38, f32[2,8,128,384]{2,3,1,0:T(8,128)} %fusion.40, ...), kind=kOutput, calls=%fused_computation.44 | convolution fusion | flops 510590976 | bytes 35520512 | tf_op jit(solution)/shard_map/bhwc,bcd->bhwd/dot_general | solution.py:48
  (126 shorter events, 68.0 us)
Async XLA Ops:
  6.5 296.3 %copy-start = (bf16[1280,320]{0,1:T(8,128)(2,1)S(1)}, bf16[1280,320]{0,1:T(8,128)(2,1)}, u32[]{:S(2)}) copy-start(bf16[1280,320]{0,1:T(8,128)(2,1)} %param.12) | copy-start | bytes 2457604
  6.5 103.9 %copy-start.5 = (bf16[2,8,128,320]{2,3,1,0:T(8,128)(2,1)S(1)}, bf16[2,8,128,320]{2,3,1,0:T(8,128)(2,1)}, u32[]{:S(2)}) copy-start(bf16[2,8,128,320]{2,3,1,0:T(8,128)(2,1)} %param.10) | copy-start | bytes 3932164
  6.5 228.4 %copy-start.15 = (f32[2,320]{1,0:T(2,128)S(1)}, f32[2,320]{1,0:T(2,128)}, u32[]{:S(2)}) copy-start(f32[2,320]{1,0:T(2,128)} %param.13) | copy-start | bytes 7684
  6.5 228.4 %copy-start.14 = (f32[2,320]{1,0:T(2,128)S(1)}, f32[2,320]{1,0:T(2,128)}, u32[]{:S(2)}) copy-start(f32[2,320]{1,0:T(2,128)} %param.14) | copy-start | bytes 7684
  6.5 318.3 %all-gather.6.cloned.1.call-start = ((), (), s32[]{:S(2)}) async-start(), calls=%async_computation | async-start | bytes 6635520 | tf_op jit(solution)/shard_map/all_gather | solution.py:80
  53.8 185.1 %copy-start.16 = (bf16[1,2,640]{2,1,0:T(2,128)(2,1)S(1)}, bf16[1,2,640]{2,1,0:T(2,128)(2,1)}, u32[]{:S(2)}) copy-start(bf16[1,2,640]{2,1,0:T(2,128)(2,1)} %param.17) | copy-start | bytes 7684
  236.4 67.0 %collective-permute-start = (bf16[2,1,128,320]{2,3,1,0:T(8,128)(2,1)S(1)}, bf16[2,1,128,320]{2,3,1,0:T(8,128)(2,1)S(1)}, u32[]{:S(2)}, u32[]{:S(2)}) collective-permute-start(bf16[2,1,128,320]{2,3,1,0:T(8,128)(2,1)S(1)} %get-tuple-element.23), channel_id=1, source_target_pairs={{0,8},{8,16},{16,24},{24,32},{32,40},{40,48},{48,56},{56,64},{64,7... | collective-permute-start | bytes 491528 | tf_op jit(solution)/shard_map/ppermute | solution.py:15
  237.7 65.7 %collective-permute-start.1 = (bf16[2,1,128,320]{2,3,1,0:T(8,128)(2,1)S(1)}, bf16[2,1,128,320]{2,3,1,0:T(8,128)(2,1)S(1)}, u32[]{:S(2)}, u32[]{:S(2)}) collective-permute-start(bf16[2,1,128,320]{2,3,1,0:T(8,128)(2,1)S(1)} %get-tuple-element.24), channel_id=1, source_target_pairs={{8,0},{16,8},{24,16},{32,24},{40,32},{48,40},{56,48},{64,56},{72,6... | collective-permute-start | bytes 491528 | tf_op jit(solution)/shard_map/ppermute | solution.py:18
  298.1 5.1 copy-start.17
  298.1 5.1 copy-start.18
  308.0 7.8 %collective-permute-start.2 = (bf16[2,10,1,320]{3,0,2,1:T(2,128)(2,1)S(1)}, bf16[2,10,1,320]{3,0,2,1:T(2,128)(2,1)S(1)}, u32[]{:S(2)}, u32[]{:S(2)}) collective-permute-start(bf16[2,10,1,320]{3,0,2,1:T(2,128)(2,1)S(1)} %copy.87), channel_id=1, source_target_pairs={{0,1},{2,3},{4,5},{6,7},{8,9},{10,11},{12,13},{14,15},{16,17},{18,... | collective-permute-start | bytes 38408 | tf_op jit(solution)/shard_map/ppermute | solution.py:15
  311.2 6.3 %collective-permute-start.3 = (bf16[2,10,1,320]{3,0,2,1:T(2,128)(2,1)S(1)}, bf16[2,10,1,320]{3,0,2,1:T(2,128)(2,1)S(1)}, u32[]{:S(2)}, u32[]{:S(2)}) collective-permute-start(bf16[2,10,1,320]{3,0,2,1:T(2,128)(2,1)S(1)} %copy.94), channel_id=1, source_target_pairs={{1,0},{3,2},{5,4},{7,6},{9,8},{11,10},{13,12},{15,14},{17,16},{19,... | collective-permute-start | bytes 38408 | tf_op jit(solution)/shard_map/ppermute | solution.py:18
  544.0 5.5 copy-start.11
  545.4 8.9 %copy-start.3 = (bf16[2,8,128,320]{2,3,1,0:T(8,128)(2,1)}, bf16[2,8,128,320]{2,3,1,0:T(8,128)(2,1)S(1)}, u32[]{:S(2)}) copy-start(bf16[2,8,128,320]{2,3,1,0:T(8,128)(2,1)S(1)} %multiply_convert_fusion) | copy-start | bytes 3932164
  545.5 7.9 %collective-permute-start.4 = (bf16[2,1,128,320]{2,3,1,0:T(8,128)(2,1)S(1)}, bf16[2,1,128,320]{2,3,1,0:T(8,128)(2,1)S(1)}, u32[]{:S(2)}, u32[]{:S(2)}) collective-permute-start(bf16[2,1,128,320]{2,3,1,0:T(8,128)(2,1)S(1)} %get-tuple-element.21), channel_id=1, source_target_pairs={{0,8},{8,16},{16,24},{24,32},{32,40},{40,48},{48,56},{56,64},{64,7... | collective-permute-start | bytes 491528 | tf_op jit(solution)/shard_map/ppermute | solution.py:15
  548.2 6.1 collective-permute-start.5
  558.8 16.8 %collective-permute-start.6 = (bf16[2,10,1,320]{3,0,2,1:T(2,128)(2,1)S(1)}, bf16[2,10,1,320]{3,0,2,1:T(2,128)(2,1)S(1)}, u32[]{:S(2)}, u32[]{:S(2)}) collective-permute-start(bf16[2,10,1,320]{3,0,2,1:T(2,128)(2,1)S(1)} %copy.104), channel_id=1, source_target_pairs={{0,1},{2,3},{4,5},{6,7},{8,9},{10,11},{12,13},{14,15},{16,17},{18,... | collective-permute-start | bytes 38408 | tf_op jit(solution)/shard_map/ppermute | solution.py:15
  560.1 12.8 %slice-start = ((s8[4423680]{0:T(1024)(128)(4,1)}), s8[229376]{0:T(1024)(128)(4,1)S(1)}, s32[]{:S(2)}) async-start(s8[4423680]{0:T(1024)(128)(4,1)} %bitcast.147), calls=%async_computation.1 | async-start | bytes 458752
  562.0 10.8 %slice-start.1 = ((s8[4423680]{0:T(1024)(128)(4,1)}), s8[4194304]{0:T(1024)(128)(4,1)S(1)}, s32[]{:S(2)}) async-start(s8[4423680]{0:T(1024)(128)(4,1)} %bitcast.147), calls=%async_computation.2 | async-start | bytes 8388608
  562.0 10.8 %copy-start.4 = (bf16[2,8,128,320]{2,3,1,0:T(8,128)(2,1)S(1)}, bf16[2,8,128,320]{2,3,1,0:T(8,128)(2,1)}, u32[]{:S(2)}) copy-start(bf16[2,8,128,320]{2,3,1,0:T(8,128)(2,1)} %copy-done.3) | copy-start | bytes 3932164
  562.1 15.2 %collective-permute-start.7 = (bf16[2,10,1,320]{3,0,2,1:T(2,128)(2,1)S(1)}, bf16[2,10,1,320]{3,0,2,1:T(2,128)(2,1)S(1)}, u32[]{:S(2)}, u32[]{:S(2)}) collective-permute-start(bf16[2,10,1,320]{3,0,2,1:T(2,128)(2,1)S(1)} %copy.109), channel_id=1, source_target_pairs={{1,0},{3,2},{5,4},{7,6},{9,8},{11,10},{13,12},{15,14},{17,16},{19,... | collective-permute-start | bytes 38408 | tf_op jit(solution)/shard_map/ppermute | solution.py:18
  577.3 6.7 %slice-start.2 = ((s8[4423680]{0:T(1024)(128)(4,1)}), s8[229376]{0:T(1024)(128)(4,1)S(1)}, s32[]{:S(2)}) async-start(s8[4423680]{0:T(1024)(128)(4,1)} %bitcast.149), calls=%async_computation.3 | async-start | bytes 458752
  597.8 8.9 %copy-start.6 = (bf16[2,8,128,320]{2,3,1,0:T(8,128)(2,1)S(1)}, bf16[2,8,128,320]{2,3,1,0:T(8,128)(2,1)}, u32[]{:S(2)}) copy-start(bf16[2,8,128,320]{2,3,1,0:T(8,128)(2,1)} %param.10) | copy-start | bytes 3932164
  597.8 10.6 %copy-start.1 = (bf16[1280,320]{0,1:T(8,128)(2,1)S(1)}, bf16[1280,320]{0,1:T(8,128)(2,1)}, u32[]{:S(2)}) copy-start(bf16[1280,320]{0,1:T(8,128)(2,1)} %param.12) | copy-start | bytes 2457604
  (8 other events, 26.5 us)
Sparse Core Ops, SparseCore 0:
  54.0 51.1 all-gather.5
